TPU v7x, 32 devices: a whole 2x2x4 slice. The times are simulated.
32 devices in a mesh: dp: 8 (over y, x, core), mp: 4 (over z).
Axes of the slice: x: 2, y: 2, z: 4, core: 2. Of those that a mesh axis runs over, the one named last changes fastest.
Arguments:
- token_block: int32 [8192, 1], P(('dp', 'mp')), may hold values from 0 to 31; in each aligned block of 256 rows (0 to 255, 256 to 511, ...) at most 16 rows name the same one
- token_offset: int32 [8192], P(('dp', 'mp')), may hold values from 0 to 15663
- lengths: int32 [128], P(('dp', 'mp')), may hold values from 1 to 64, as said below
- group_counts: int32 [109], replicated, may hold values from 1 to 16, 128 in all
- table: bfloat16 [501248, 768], P(('dp', 'mp')), may hold values from -6 to 6
- weight_qkv: bfloat16 [768, 2304], P(None, 'mp'), may hold values from -0.21875 to 0.21875
- bias_query: bfloat16 [768], P('mp'), may hold values from -2 to 2
- bias_value: bfloat16 [768], P('mp'), may hold values from -2 to 2
- weight_out: bfloat16 [768, 768], P('mp'), may hold values from -0.875 to 0.875
- bias_out: bfloat16 [768], replicated, may hold values from -2 to 2
- gain_one: bfloat16 [768], replicated, may hold values from 0.5 to 1.5
- shift_one: bfloat16 [768], replicated, may hold values from -2 to 2
- weight_in: bfloat16 [768, 3072], P(None, 'mp'), may hold values from -0.21875 to 0.21875
- bias_in: bfloat16 [3072], P('mp'), may hold values from -2 to 2
- weight_down: bfloat16 [3072, 768], P('mp'), may hold values from -0.15625 to 0.15625
- bias_down: bfloat16 [768], replicated, may hold values from -2 to 2
- gain_two: bfloat16 [768], replicated, may hold values from 0.5 to 1.5
- shift_two: bfloat16 [768], replicated, may hold values from -2 to 2
- cotangent: bfloat16 [8192, 768], P(('dp', 'mp')), may hold values from -6 to 6
Outputs:
- activations: bfloat16 [8192, 768], P(('dp', 'mp'))
- grad_table: float32 [501248, 768], P(('dp', 'mp'))
- grad_weight_qkv: float32 [768, 2304], P(None, 'mp')
- grad_bias_query: float32 [768], P('mp')
- grad_bias_value: float32 [768], P('mp')
- grad_weight_out: float32 [768, 768], P('mp')
- grad_bias_out: float32 [768], replicated
- grad_gain_one: float32 [768], replicated
- grad_shift_one: float32 [768], replicated
- grad_weight_in: float32 [768, 3072], P(None, 'mp')
- grad_bias_in: float32 [3072], P('mp')
- grad_weight_down: float32 [3072, 768], P('mp')
- grad_bias_down: float32 [768], replicated
- grad_gain_two: float32 [768], replicated
- grad_shift_two: float32 [768], replicated
Inputs may be any that keep to these rules, and one draw needn't show every extreme that they name: `token_block`: among the rows of one device, at most 16 tokens name the same block. `lengths`: positions from a sentence's length on are padding. `group_counts`: the counts sum to 128.
All inputs are finite; a program needn't handle non-finite values.
Results may differ from a plain program's by a relative error of at most 0.02.
Values may be sent and summed in bfloat16 or wider, within the bound.
A program may use at most 192 MiB of HBM per device.

v0:
```python
from functools import partial
import jax
import jax.numpy as jnp
from jax import lax
from jax.sharding import PartitionSpec as P

HD = 64
SEQ = 64
eps_norm = 1e-12


def norm_rows(hidden, gain_vec, shift_vec):
    row_mean = jnp.mean(hidden, axis=-1, keepdims=True)
    centred = hidden - row_mean
    variance = jnp.mean(centred * centred, axis=-1, keepdims=True)
    row_scale = lax.rsqrt(variance + eps_norm)
    normed = centred * row_scale
    return (normed * gain_vec + shift_vec, normed, row_scale)


def norm_back(grad_out, normed, row_scale, gain_vec):
    grad_normed = grad_out * gain_vec
    inner_mean = jnp.mean(grad_normed, axis=-1, keepdims=True)
    cross_mean = jnp.mean(grad_normed * normed, axis=-1, keepdims=True)
    grad_in = row_scale * (grad_normed - inner_mean - normed * cross_mean)
    return (grad_in, jnp.sum(grad_out * normed, axis=0), jnp.sum(grad_out, axis=0))


def on_device(
    token_block,
    token_offset,
    lengths,
    group_counts,
    table,
    weight_qkv,
    bias_query,
    bias_value,
    weight_out,
    bias_out,
    gain_one,
    shift_one,
    weight_in,
    bias_in,
    weight_down,
    bias_down,
    gain_two,
    shift_two,
    cotangent,
):
    f32 = jnp.float32
    bf16 = jnp.bfloat16
    devices = lax.axis_size(("dp", "mp"))
    tok_rows = token_offset.shape[0]
    model_width = table.shape[1]
    capacity = max(2, 2 * tok_rows // devices)
    token_owner = token_block[:, 0]
    owner_hits = (token_owner[:, None] == jnp.arange(devices, dtype=jnp.int32)[None, :]).astype(
        jnp.int32
    )
    slot_index = jnp.sum((jnp.cumsum(owner_hits, axis=0) - 1) * owner_hits, axis=1)
    slot_place = token_owner * capacity + slot_index
    requests = jnp.full((devices * capacity,), -1, jnp.int32).at[slot_place].set(token_offset)
    wanted = lax.all_to_all(
        requests.reshape(devices, capacity), ("dp", "mp"), split_axis=0, concat_axis=0, tiled=True
    )
    slot_live = wanted >= 0
    wanted_rows = jnp.maximum(wanted, 0)
    fetched = lax.all_to_all(
        table[wanted_rows], ("dp", "mp"), split_axis=0, concat_axis=0, tiled=True
    )
    embedded = fetched.reshape(devices * capacity, model_width)[slot_place]
    sent_local = lengths.shape[0]
    total_sent = sent_local * devices
    group_num = group_counts.shape[0]
    sent_index = lax.axis_index(("dp", "mp")) * sent_local + jnp.arange(sent_local, dtype=jnp.int32)
    offsets = jnp.cumsum(group_counts) - group_counts
    member = (sent_index[:, None] >= offsets[None, :]) & (
        sent_index[:, None] < (offsets + group_counts)[None, :]
    )
    group_weight = total_sent / (group_num * group_counts.astype(f32))
    sent_weight = jnp.sum(jnp.where(member, group_weight[None, :], f32(0.0)), axis=1)
    positions = jnp.arange(SEQ, dtype=f32)
    token_live = (positions[None, :] < lengths[:, None].astype(f32)).astype(f32)
    row_weight = (token_live * sent_weight[:, None]).reshape(tok_rows)
    count_local = jnp.sum(lengths).astype(f32)
    whole_in, whole_len = (
        lax.all_gather(embedded, "mp", axis=0, tiled=True),
        lax.all_gather(lengths.astype(bf16), "mp", axis=0, tiled=True),
    )
    rows_all = whole_in.shape[0]
    sentences_all = whole_len.shape[0]
    head_count = weight_qkv.shape[1] // (3 * HD)
    block_sent = min(8, sentences_all)
    block_count = sentences_all // block_sent
    mixed_qkv = jnp.dot(whole_in, weight_qkv, preferred_element_type=f32).reshape(
        rows_all, head_count, 3, HD
    )
    block_shape = (block_count, block_sent, SEQ, head_count, HD)
    queries = (
        (mixed_qkv[:, :, 0, :] + bias_query.astype(f32).reshape(head_count, HD))
        .astype(bf16)
        .reshape(block_shape)
    )
    key_rows = mixed_qkv[:, :, 1, :].astype(bf16).reshape(block_shape)
    value_rows = (
        (mixed_qkv[:, :, 2, :] + bias_value.astype(f32).reshape(head_count, HD))
        .astype(bf16)
        .reshape(block_shape)
    )
    len_blocks = whole_len.astype(f32).reshape(block_count, block_sent)

    def block_scores(q_blk, k_blk, len_blk):
        scores = jnp.einsum("sqhe,skhe->shqk", q_blk, k_blk, preferred_element_type=f32) * 0.125
        key_valid = positions[None, :] < len_blk[:, None]
        return jnp.where(key_valid[:, None, None, :], scores, f32(-1e30))

    def attend(block_items):
        q_blk, k_blk, v_blk, len_blk = block_items
        scores = block_scores(q_blk, k_blk, len_blk)
        row_max = jnp.max(scores, axis=-1, keepdims=True)
        exp_total = jnp.sum(jnp.exp(scores - row_max), axis=-1, keepdims=True)
        log_total = row_max + jnp.log(exp_total)
        attn_probs = jnp.exp(scores - log_total)
        context_blk = jnp.einsum(
            "shqk,skhe->sqhe", attn_probs.astype(bf16), v_blk, preferred_element_type=f32
        ).astype(bf16)
        return (context_blk, log_total[..., 0])

    context_blocks, log_totals = lax.map(attend, (queries, key_rows, value_rows, len_blocks))
    context = context_blocks.reshape(rows_all, head_count * HD)
    attn_sum = lax.psum_scatter(
        jnp.dot(context, weight_out, preferred_element_type=f32),
        "mp",
        scatter_dimension=0,
        tiled=True,
    )
    gain_one_f = gain_one.astype(f32)
    gain_two_f = gain_two.astype(f32)
    first_out, normed_one, scale_one = norm_rows(
        embedded.astype(f32) + attn_sum + bias_out.astype(f32), gain_one_f, shift_one.astype(f32)
    )
    whole_first = lax.all_gather(first_out.astype(bf16), "mp", axis=0, tiled=True)
    hidden_pre = jnp.dot(whole_first, weight_in, preferred_element_type=f32) + bias_in.astype(f32)
    gelu_val, gelu_pull = jax.vjp(partial(jax.nn.gelu, approximate=False), hidden_pre)
    hidden_act = gelu_val.astype(bf16)
    down_sum = lax.psum_scatter(
        jnp.dot(
            lax.slice_in_dim(hidden_act, 0, tok_rows * lax.axis_size("mp"), axis=0),
            weight_down,
            preferred_element_type=f32,
        ),
        "mp",
        scatter_dimension=0,
        tiled=True,
    )
    final_out, normed_two, scale_two = norm_rows(
        first_out + down_sum + bias_down.astype(f32), gain_two_f, shift_two.astype(f32)
    )
    activations = final_out.astype(bf16)
    grad_final = row_weight[:, None] * cotangent.astype(f32)
    grad_h2, grad_gain_two, grad_shift_two = norm_back(
        grad_final, normed_two, scale_two, gain_two_f
    )
    grad_bias_down = jnp.sum(grad_h2, axis=0)
    whole_grad_down = lax.all_gather(grad_h2.astype(bf16), "mp", axis=0, tiled=True)
    grad_weight_down = jnp.einsum(
        "rf,rd->fd", hidden_act, whole_grad_down, preferred_element_type=f32
    )
    grad_act = jnp.einsum("rd,fd->rf", whole_grad_down, weight_down, preferred_element_type=f32)
    grad_pre = gelu_pull(grad_act)[0].astype(bf16)
    grad_bias_in = jnp.sum(grad_pre.astype(f32), axis=0)
    grad_weight_in = jnp.einsum("rd,rf->df", whole_first, grad_pre, preferred_element_type=f32)
    grad_first = grad_h2 + lax.psum_scatter(
        jnp.einsum("rf,df->rd", grad_pre, weight_in, preferred_element_type=f32),
        "mp",
        scatter_dimension=0,
        tiled=True,
    )
    grad_h1, grad_gain_one, grad_shift_one = norm_back(
        grad_first, normed_one, scale_one, gain_one_f
    )
    grad_bias_out = jnp.sum(grad_h1, axis=0)
    whole_grad_attn = lax.all_gather(grad_h1.astype(bf16), "mp", axis=0, tiled=True)
    grad_weight_out = jnp.einsum("rc,rd->cd", context, whole_grad_attn, preferred_element_type=f32)
    grad_context = (
        jnp.einsum("rd,cd->rc", whole_grad_attn, weight_out, preferred_element_type=f32)
        .astype(bf16)
        .reshape(block_shape)
    )

    def attend_back(block_items):
        q_blk, k_blk, v_blk, len_blk, log_blk, dctx_blk = block_items
        scores = block_scores(q_blk, k_blk, len_blk)
        attn_probs = jnp.exp(scores - log_blk[..., None])
        grad_probs = jnp.einsum("sqhe,skhe->shqk", dctx_blk, v_blk, preferred_element_type=f32)
        grad_value = jnp.einsum(
            "shqk,sqhe->skhe", attn_probs.astype(bf16), dctx_blk, preferred_element_type=f32
        ).astype(bf16)
        grad_scores = (
            attn_probs * (grad_probs - jnp.sum(grad_probs * attn_probs, axis=-1, keepdims=True))
        ).astype(bf16)
        grad_query = (
            jnp.einsum("shqk,skhe->sqhe", grad_scores, k_blk, preferred_element_type=f32) * 0.125
        ).astype(bf16)
        grad_key = (
            jnp.einsum("shqk,sqhe->skhe", grad_scores, q_blk, preferred_element_type=f32) * 0.125
        ).astype(bf16)
        return jnp.stack([grad_query, grad_key, grad_value], axis=3)

    grad_mixed = lax.map(
        attend_back, (queries, key_rows, value_rows, len_blocks, log_totals, grad_context)
    )
    grad_mixed = grad_mixed.reshape(rows_all, head_count * 3 * HD)
    grad_weight_qkv = jnp.einsum("rd,rc->dc", whole_in, grad_mixed, preferred_element_type=f32)
    grad_parts = jnp.sum(grad_mixed.astype(f32).reshape(rows_all, head_count, 3, HD), axis=0)
    grad_bias_query = grad_parts[:, 0, :].reshape(head_count * HD)
    grad_bias_value = grad_parts[:, 2, :].reshape(head_count * HD)
    grad_embed = grad_h1 + lax.psum_scatter(
        jnp.einsum("rc,dc->rd", grad_mixed, weight_qkv, preferred_element_type=f32).astype(
            jnp.bfloat16
        ),
        "mp",
        scatter_dimension=0,
        tiled=True,
    ).astype(jnp.float32)
    (
        count_all,
        sum_gain_one,
        sum_shift_one,
        sum_bias_out,
        sum_gain_two,
        sum_shift_two,
        sum_bias_down,
    ) = lax.psum(
        (
            count_local,
            grad_gain_one,
            grad_shift_one,
            grad_bias_out,
            grad_gain_two,
            grad_shift_two,
            grad_bias_down,
        ),
        ("dp", "mp"),
    )
    factor = lax.rsqrt(count_all)
    sum_qkv, sum_query, sum_value, sum_out, sum_in, sum_bias_in, sum_down = (
        lax.psum(grad_weight_qkv.astype(jnp.bfloat16), "dp").astype(jnp.float32),
        lax.psum(grad_bias_query.astype(jnp.bfloat16), "dp").astype(jnp.float32),
        lax.psum(grad_bias_value.astype(jnp.bfloat16), "dp").astype(jnp.float32),
        lax.psum(grad_weight_out.astype(jnp.bfloat16), "dp").astype(jnp.float32),
        lax.psum(grad_weight_in.astype(jnp.bfloat16), "dp").astype(jnp.float32),
        lax.psum(grad_bias_in.astype(jnp.bfloat16), "dp").astype(jnp.float32),
        lax.psum(grad_weight_down.astype(jnp.bfloat16), "dp").astype(jnp.float32),
    )
    outgoing = (
        jnp.zeros((devices * capacity, model_width), f32)
        .at[slot_place]
        .set(grad_embed)
        .reshape(devices, capacity, model_width)
    )
    incoming = lax.all_to_all(
        outgoing.astype(jnp.bfloat16), ("dp", "mp"), split_axis=0, concat_axis=0, tiled=True
    ).astype(outgoing.dtype)
    received = jnp.where(slot_live[..., None], incoming, f32(0.0)).reshape(
        devices * capacity, model_width
    )
    grad_table = jnp.zeros(table.shape, f32).at[wanted_rows.reshape(-1)].add(received) * factor
    return (
        activations,
        grad_table,
        sum_qkv * factor,
        sum_query * factor,
        sum_value * factor,
        sum_out * factor,
        sum_bias_out * factor,
        sum_gain_one * factor,
        sum_shift_one * factor,
        sum_in * factor,
        sum_bias_in * factor,
        sum_down * factor,
        sum_bias_down * factor,
        sum_gain_two * factor,
        sum_shift_two * factor,
    )


def solution(mesh):
    placed = (
        P(("dp", "mp"), None),
        P(("dp", "mp")),
        P(("dp", "mp")),
        P(),
        P(("dp", "mp"), None),
        P(None, "mp"),
        P("mp"),
        P("mp"),
        P("mp", None),
        P(),
        P(),
        P(),
        P(None, "mp"),
        P("mp"),
        P("mp", None),
        P(),
        P(),
        P(),
        P(("dp", "mp"), None),
    )
    return jax.shard_map(
        on_device,
        mesh=mesh,
        in_specs=placed,
        out_specs=(
            P(("dp", "mp"), None),
            P(("dp", "mp"), None),
            P(None, "mp"),
            P("mp"),
            P("mp"),
            P("mp", None),
            P(),
            P(),
            P(),
            P(None, "mp"),
            P("mp"),
            P("mp", None),
            P(),
            P(),
            P(),
        ),
        check_vma=False,
    )
```

profile of v0, /device:TPU:0, one launch (start us, length us, event | category | flops | bytes accessed | tf_op | source)
XLA Modules:
  0.0 689.7 jit_solution(15730359723597608846)
XLA Ops:
  11.9 14.3 %all_to_all.19 = s32[32,1,16]{2,1,0:T(1,128)S(1)} all-to-all(s32[32,1,16]{2,1,0:T(1,128)S(1)} %bitcast.198), channel_id=1, replica_groups=mesh['dp'=8,'mp'=4] {'dp','mp'}, dimensions={0} | all-to-all | bytes 4096 | tf_op jit(solution)/shard_map/all_to_all | solution.py:63
  26.5 14.0 %gather_fusion = bf16[512,768]{1,0:T(8,128)(2,1)} fusion(bf16[15664,768]{1,0:T(8,128)(2,1)} %param.27, s32[1024]{0:T(1024)S(1)} %pad_clamp_fusion.1), kind=kCustom, calls=%fused_computation | custom fusion | bytes 1574912 | tf_op jit(solution)/shard_map/gather | solution.py:69
  43.4 19.4 %all-to-all-done.1 = bf16[32,16,768]{2,1,0:T(8,128)(2,1)S(1)} async-done(((bf16[32,16,768]{2,1,0:T(8,128)(2,1)}), bf16[32,16,768]{2,1,0:T(8,128)(2,1)S(1)}, u32[]{:S(2)}, u32[]{:S(2)}) %all-to-all-start.1) | async-done | bytes 786464 | tf_op jit(solution)/shard_map/all_to_all | solution.py:68
  67.4 11.9 %all-reduce = bf16[16]{0:T(256)(128)(2,1)S(1)} all-reduce(bf16[16]{0:T(256)(128)(2,1)S(1)} %dynamic-update-slice), channel_id=1, replica_groups=mesh['dp'=8,'mp'=4] {'mp'}, use_global_device_ids=true, to_apply=%add | all-reduce | flops 16 | bytes 64
  80.2 21.7 %all-gather.12.cloned.1.call-done = bf16[1024,768]{1,0:T(8,128)(2,1)} async-done(((bf16[256,768]{1,0:T(8,128)(2,1)}), bf16[1024,768]{1,0:T(8,128)(2,1)}) %all-gather.12.cloned.1.call-update) | async-done | bytes 1572880 | tf_op jit(solution)/shard_map/all_gather | solution.py:87
  115.4 4.8 while.24
  128.3 57.3 %reduce-scatter.5.cloned.1.call-done = f32[256,768]{1,0:T(8,128)} async-done(((f32[1024,768]{1,0:T(8,128)}), f32[256,768]{1,0:T(8,128)}) %reduce-scatter.5.cloned.1.call-update) | async-done | bytes 786448 | tf_op jit(solution)/shard_map/reduce_scatter | solution.py:131
  191.0 35.6 %all-gather.6.cloned.1.call-done = bf16[1024,768]{1,0:T(8,128)(2,1)} async-done(((bf16[256,768]{1,0:T(8,128)(2,1)}), bf16[1024,768]{1,0:T(8,128)(2,1)}) %all-gather.6.cloned.1.call-update) | async-done | bytes 1572880 | tf_op jit(solution)/shard_map/all_gather | solution.py:142
  226.6 10.6 %multiply_convert_fusion.1 = (bf16[1024,768]{1,0:T(8,128)(2,1)S(1)}, f32[1024,768]{1,0:T(8,128)}, f32[1024,768]{1,0:T(8,128)}) fusion(f32[768]{0:T(1024)} %convert_element_type.189, bf16[1024,768]{1,0:T(8,128)(2,1)} %all-gather.6.cloned.1.call-done, bf16[768,768]{1,0:T(8,128)(2,1)S(1)} %copy-done), kind=kOutput, calls=%fused_computation.71 | convolution fusion | flops 1259864064 | bytes 10619904 | tf_op jit(solution)/shard_map/dot_general | solution.py:143
  254.6 46.3 %reduce-scatter.7.cloned.1.call-done = f32[256,768]{1,0:T(8,128)} async-done(((f32[1024,768]{1,0:T(8,128)}), f32[256,768]{1,0:T(8,128)}) %reduce-scatter.7.cloned.1.call-update) | async-done | bytes 786448 | tf_op jit(solution)/shard_map/reduce_scatter | solution.py:146
  307.2 37.0 %all-gather.8.cloned.1.call-done = bf16[1024,768]{1,0:T(8,128)(2,1)} async-done(((bf16[256,768]{1,0:T(8,128)(2,1)}), bf16[1024,768]{1,0:T(8,128)(2,1)}) %all-gather.8.cloned.1.call-update) | async-done | bytes 1572880 | tf_op jit(solution)/shard_map/all_gather | solution.py:165
  344.3 6.4 fusion.61
  355.0 59.4 %reduce-scatter.9.cloned.1.call-done = f32[256,768]{1,0:T(8,128)} async-done(((f32[1024,768]{1,0:T(8,128)}), f32[256,768]{1,0:T(8,128)}) %reduce-scatter.9.cloned.1.call-update) | async-done | bytes 786448 | tf_op jit(solution)/shard_map/reduce_scatter | solution.py:173
  418.8 36.6 %all-gather.10.cloned.1.call-done = bf16[1024,768]{1,0:T(8,128)(2,1)} async-done(((bf16[256,768]{1,0:T(8,128)(2,1)}), bf16[1024,768]{1,0:T(8,128)(2,1)}) %all-gather.10.cloned.1.call-update) | async-done | bytes 1572880 | tf_op jit(solution)/shard_map/all_gather | solution.py:183
  458.0 16.8 %while.25 = (s32[]{:T(128)}, bf16[2,8,64,3,3,64]{5,2,3,1,4,0:T(8,128)(2,1)}, bf16[2,8,64,3,64]{4,2,3,1,0:T(8,128)(2,1)S(1)}, f32[2,8]{1,0:T(2,128)S(1)}, bf16[2,...) while((s32[]{:T(128)}, ...), condition=%wide.region_23.24_spmd.clone, body=%wide.region_21.23_spmd.clone.sunk | while | flops 66059264 | bytes 22653772 | solution.py:210
  474.8 3.5 copy.153
  481.0 4.2 convolution_convert_fusion.2
  486.0 4.0 convolution_convert_fusion.3
  492.6 41.3 %all-reduce.1 = (f32[]{:T(128)}, f32[768]{0:T(1024)S(1)}, f32[768]{0:T(1024)S(1)}, f32[768]{0:T(1024)S(1)}, f32[768]{0:T(1024)S(1)}, /*index=5*/f32[768]{0:T(1024)S(1)}, f32[768]{0:T(1024)S(1)}) all-reduce(f32[]{:T(128)S(6)} %convert_element_type.207, f32[768]{0:T(1024)S(1)} %copy-done.29, ...), channel_id=1, replica_groups=mesh['dp'=8,'mp'=4] {'dp','mp'}, use_global_device_ids=true, to_apply=%region_28.29 | all-reduce | flops 4609 | bytes 36872 | tf_op jit(solution)/shard_map/psum | solution.py:234
  537.0 3.8 convolution_convert_fusion.5
  544.0 13.8 %all-reduce.2 = (bf16[192]{0:T(256)(128)(2,1)S(1)}, bf16[192]{0:T(256)(128)(2,1)S(1)}, bf16[768]{0:T(1024)(128)(2,1)S(1)}) all-reduce(bf16[192]{0:T(256)(128)(2,1)S(1)} %convert_element_type.211, bf16[192]{0:T(256)(128)(2,1)S(1)} %convert_element_type.213, bf16[768]{0:T(1024)(128)(2,1)S(1)} %copy-done.35), channel_id=1, replica_groups=mesh['dp'=8,'mp'=4] {'dp'}, use_global_device_ids=true, to_apply=%region_31.32 | all-reduce | flops 1152 | bytes 4608 | tf_op jit(solution)/shard_map/psum | solution.py:249
  565.9 52.4 %all-reduce.6.cloned.1.call-done = (bf16[768,576]{0,1:T(8,128)(2,1)}, bf16[192,768]{1,0:T(8,128)(2,1)}, bf16[768,768]{1,0:T(8,128)(2,1)}, bf16[768,768]{1,0:T(8,128)(2,1)}) async-done(((bf16[768,576]{0,1:T(8,128)(2,1)}, bf16[192,768]{1,0:T(8,128)(2,1)}, bf16[768,768]{1,0:T(8,128)(2,1)}, bf16[768,768]{1,0:T(8,128)(2,1)}), (bf16[768,576]{0,1:T(8,128)(2,1)}, bf16[192,768]{1,0:T(8,128)(2,1)}, ...) | async-done | bytes 3538960 | tf_op jit(solution)/shard_map/psum | solution.py:248
  626.1 23.7 %scatter_custom_fusion.2 = f32[15664,768]{1,0:T(8,128)} fusion(s32[512]{0:T(512)} %copy-done.32, f32[512,768]{1,0:T(8,128)S(1)} %bitcast.197, f32[]{:T(128)} %constant.48.clone.1), kind=kCustom, calls=%fused_computation.66 | custom fusion | flops 393216 | bytes 48120320 | tf_op jit(solution)/shard_map/scatter-add | solution.py:268
  649.8 33.1 %broadcast_multiply_fusion = f32[15664,768]{1,0:T(8,128)} fusion(f32[15664,768]{1,0:T(8,128)} %scatter_custom_fusion.2, f32[]{:T(128)S(6)} %rsqrt.21), kind=kLoop, calls=%fused_computation.65 | loop fusion | flops 12029952 | bytes 96239616 | tf_op jit(solution)/shard_map/mul | solution.py:268
  (278 shorter events, 122.4 us)
Async XLA Ops:
  7.2 219.4 %copy-start = (bf16[768,768]{1,0:T(8,128)(2,1)S(1)}, bf16[768,768]{1,0:T(8,128)(2,1)}, u32[]{:S(2)}) copy-start(bf16[768,768]{1,0:T(8,128)(2,1)} %param.35) | copy-start | bytes 3538948
  10.2 33.1 %copy-start.33 = (s32[256,1]{0,1:T(1,128)}, s32[256,1]{0,1:T(1,128)S(1)}, u32[]{:S(2)}) copy-start(s32[256,1]{0,1:T(1,128)S(1)} %compare_select_fusion) | copy-start | bytes 3076
  40.5 24.3 %copy-start.44 = (u32[32]{0:T(128)S(1)}, u32[32]{0:T(128)}, u32[]{:S(2)}) copy-start(u32[32]{0:T(128)} %constant.171) | copy-start | bytes 388
  40.5 25.6 %copy-start.38 = (s32[4]{0:T(128)S(1)}, s32[4]{0:T(128)}, u32[]{:S(2)}) copy-start(s32[4]{0:T(128)} %param.25) | copy-start | bytes 52
  40.5 39.5 %copy-start.36 = (bf16[192]{0:T(256)(128)(2,1)S(1)}, bf16[192]{0:T(256)(128)(2,1)}, u32[]{:S(2)}) copy-start(bf16[192]{0:T(256)(128)(2,1)} %param.29) | copy-start | bytes 1156
  40.5 39.6 %copy-start.37 = (bf16[192]{0:T(256)(128)(2,1)S(1)}, bf16[192]{0:T(256)(128)(2,1)}, u32[]{:S(2)}) copy-start(bf16[192]{0:T(256)(128)(2,1)} %param.30) | copy-start | bytes 1156
  40.5 22.3 %all-to-all-start.1 = ((bf16[32,16,768]{2,1,0:T(8,128)(2,1)}), bf16[32,16,768]{2,1,0:T(8,128)(2,1)S(1)}, u32[]{:S(2)}, u32[]{:S(2)}) async-start(bf16[32,16,768]{2,1,0:T(8,128)(2,1)} %bitcast.6), calls=%async_computation.1 | async-start | bytes 1572864 | tf_op jit(solution)/shard_map/all_to_all | solution.py:68
  43.3 58.5 %all-gather.12.cloned.1.call-start = ((), (), s32[]{:S(2)}) async-start(), calls=%async_computation.14 | async-start | bytes 1966080 | tf_op jit(solution)/shard_map/all_gather | solution.py:87
  64.7 120.9 %reduce-scatter.5.cloned.1.call-start = ((), (), s32[]{:S(2)}) async-start(), calls=%async_computation.7 | async-start | bytes 3932160 | tf_op jit(solution)/shard_map/reduce_scatter | solution.py:131
  126.3 100.3 %all-gather.6.cloned.1.call-start = ((), (), s32[]{:S(2)}) async-start(), calls=%async_computation.8 | async-start | bytes 1966080 | tf_op jit(solution)/shard_map/all_gather | solution.py:142
  189.5 111.4 %reduce-scatter.7.cloned.1.call-start = ((), (), s32[]{:S(2)}) async-start(), calls=%async_computation.9 | async-start | bytes 3932160 | tf_op jit(solution)/shard_map/reduce_scatter | solution.py:146
  241.5 102.7 %all-gather.8.cloned.1.call-start = ((), (), s32[]{:S(2)}) async-start(), calls=%async_computation.10 | async-start | bytes 1966080 | tf_op jit(solution)/shard_map/all_gather | solution.py:165
  307.2 107.2 %reduce-scatter.9.cloned.1.call-start = ((), (), s32[]{:S(2)}) async-start(), calls=%async_computation.11 | async-start | bytes 3932160 | tf_op jit(solution)/shard_map/reduce_scatter | solution.py:173
  354.9 59.5 %copy-start.11 = (f32[256,768]{1,0:T(8,128)S(1)}, f32[256,768]{1,0:T(8,128)}, u32[]{:S(2)}) copy-start(f32[256,768]{1,0:T(8,128)} %copy-done.10) | copy-start | bytes 2359300
  354.9 59.5 %copy-start.23 = (f32[256]{0:T(256)S(1)}, f32[256]{0:T(256)}, u32[]{:S(2)}) copy-start(f32[256]{0:T(256)} %copy-done.22) | copy-start | bytes 3076
  354.9 100.5 %all-gather.10.cloned.1.call-start = ((), (), s32[]{:S(2)}) async-start(), calls=%async_computation.12 | async-start | bytes 1966080 | tf_op jit(solution)/shard_map/all_gather | solution.py:183
  417.4 38.0 %copy-start.8 = (f32[256,768]{1,0:T(8,128)}, f32[256,768]{1,0:T(8,128)S(1)}, u32[]{:S(2)}) copy-start(f32[256,768]{1,0:T(8,128)S(1)} %get-tuple-element.276) | copy-start | bytes 2359300
  417.4 40.6 %copy-start.43 = (f32[2,8]{1,0:T(2,128)S(1)}, f32[2,8]{1,0:T(2,128)}, u32[]{:S(2)}) copy-start(f32[2,8]{1,0:T(2,128)} %reshape.323) | copy-start | bytes 196
  418.3 140.0 %reduce-scatter.11.cloned.1.call-start = ((), (), s32[]{:S(2)}) async-start(), calls=%async_computation.13 | async-start | bytes 1966080 | tf_op jit(solution)/shard_map/reduce_scatter | solution.py:218
  485.2 133.0 %all-reduce.6.cloned.1.call-start = ((), (), s32[]{:S(2)}) async-start(), calls=%async_computation.15 | async-start | bytes 7077888 | tf_op jit(solution)/shard_map/psum | solution.py:248
  490.1 45.7 %copy-start.12 = (bf16[1024,192]{0,1:T(8,128)(2,1)S(1)}, bf16[1024,192]{0,1:T(8,128)(2,1)}, u32[]{:S(2)}) copy-start(bf16[1024,192]{0,1:T(8,128)(2,1)} %reshape.315) | copy-start | bytes 1179652
  490.1 45.7 %copy-start.13 = (bf16[1024,768]{1,0:T(8,128)(2,1)S(1)}, bf16[1024,768]{1,0:T(8,128)(2,1)}, u32[]{:S(2)}) copy-start(bf16[1024,768]{1,0:T(8,128)(2,1)} %all-gather.10.cloned.1.call-done) | copy-start | bytes 4718596
  561.6 64.2 %all-to-all-start.2 = ((bf16[32,16,768]{2,1,0:T(8,128)(2,1)}), bf16[32,16,768]{2,1,0:T(8,128)(2,1)S(1)}, u32[]{:S(2)}, u32[]{:S(2)}) async-start(bf16[32,16,768]{2,1,0:T(8,128)(2,1)} %bitcast.12), calls=%async_computation.6 | async-start | bytes 1572864 | tf_op jit(solution)/shard_map/all_to_all | solution.py:262
  649.8 33.1 %copy-start.1 = (bf16[768,768]{1,0:T(8,128)(2,1)S(1)}, bf16[768,768]{1,0:T(8,128)(2,1)}, u32[]{:S(2)}) copy-start(bf16[768,768]{1,0:T(8,128)(2,1)} %param.35) | copy-start | bytes 3538948
  (43 other events, 135.5 us)
Sparse Core Ops, SparseCore 0:
  64.8 36.9 all-gather.11
  126.4 59.2 reduce-scatter.4
  189.6 36.9 all-gather.5
  241.6 59.2 reduce-scatter.6
  307.3 36.9 all-gather.7
  355.1 59.2 reduce-scatter.8
  418.4 36.9 all-gather.9
  485.3 35.0 reduce-scatter.10
  540.9 77.2 all-reduce.5
where the time goes:
time: 697 us; the launch traced here: 690 us
  waiting for transfers between devices  366 us (53%)
  other arithmetic  109 us (16%)
  blocking collectives  81.4 us (12%)
  local copies, waits for them, and re-layouts  58.3 us (8%)
  matrix products  51.5 us (7%)
  between operations  16.5 us (2%)
    reduce_scatter x1, waiting for transfers between devices, on_device(): lax.psum_scatter(jnp.einsum('rf,df->rd', grad_pre, weight_in, preferred_e...  59.4 us
    reduce_scatter x1, waiting for transfers between devices, on_device(): lax.psum_scatter(jnp.dot(context, weight_out, preferred_element_type=f32)...  57.3 us
    psum x1, waiting for transfers between devices, on_device(): lax.psum(grad_weight_qkv.astype(jnp.bfloat16), 'dp').astype(jnp.float32)  52.4 us
    reduce_scatter x1, waiting for transfers between devices, on_device(): lax.psum_scatter(jnp.dot(lax.slice_in_dim(hidden_act, 0, tok_rows * lax.a...  46.3 us
    psum x1, blocking collectives, on_device(): lax.psum((count_local, grad_gain_one, grad_shift_one, grad_bias_out, grad...  41.3 us
    all_gather x1, waiting for transfers between devices, on_device(): lax.all_gather(grad_h2.astype(bf16), 'mp', axis=0, tiled=True)  37 us
    all_gather x1, waiting for transfers between devices, on_device(): lax.all_gather(grad_h1.astype(bf16), 'mp', axis=0, tiled=True)  36.6 us
    all_gather x1, waiting for transfers between devices, on_device(): lax.all_gather(first_out.astype(bf16), 'mp', axis=0, tiled=True)  35.6 us
  transfers between devices with their start and end apart: 11, of which 9 were waited for; matrix products, arithmetic and copies ran while one was open for 7% of the time, Pallas kernels for 0%

commit v1 on v0

--- a/solution.py
+++ b/solution.py
@@ -1,3 +1,4 @@
+import functools
 from functools import partial
 import jax
 import jax.numpy as jnp
@@ -7,6 +8,16 @@
 HD = 64
 SEQ = 64
 eps_norm = 1e-12
+
+
+def _wait_limits(obj, mesh_dim):
+    tray = []
+    for _ in range(lax.axis_size(mesh_dim)):
+        tray.append(obj)
+    return jnp.concatenate(lax.all_to_all(jnp.stack(tray), mesh_dim, 0, 0), axis=0)
+
+
+cut_kinds_up = functools.partial(_wait_limits, mesh_dim="mp")
 
 
 def norm_rows(hidden, gain_vec, shift_vec):
@@ -162,7 +173,7 @@
         grad_final, normed_two, scale_two, gain_two_f
     )
     grad_bias_down = jnp.sum(grad_h2, axis=0)
-    whole_grad_down = lax.all_gather(grad_h2.astype(bf16), "mp", axis=0, tiled=True)
+    whole_grad_down = cut_kinds_up(grad_h2.astype(bf16))
     grad_weight_down = jnp.einsum(
         "rf,rd->fd", hidden_act, whole_grad_down, preferred_element_type=f32
     )

time: 697 us -> 699 us (level)
  blocking collectives: 81.4 us -> 122 us
  waiting for transfers between devices: 366 us -> 329 us
    all_to_all x0 -> x1, blocking collectives: none -> 40.6 us  [_wait_limits(): lax.all_to_all(jnp.stack(tray), mesh_dim, 0, 0)]
    all_gather x1 -> x0, waiting for transfers between devices: 37 us -> none  [on_device(): lax.all_gather(grad_h2.astype(bf16), 'mp', axis=0, tiled=True)]
  transfers between devices with their start and end apart: 11 -> 10, of which waited for: 9 -> 8; matrix products, arithmetic and copies ran while one was open for 7% -> 7% of each run, Pallas kernels for 0% -> 0%
where the time goes in v1:
time: 699 us; the launch traced here: 691 us
  waiting for transfers between devices  329 us (47%)
  blocking collectives  122 us (17%)
  other arithmetic  109 us (16%)
  local copies, waits for them, and re-layouts  60.4 us (9%)
  matrix products  46.9 us (7%)
  between operations  16.9 us (2%)
    reduce_scatter x1, waiting for transfers between devices, on_device(): lax.psum_scatter(jnp.einsum('rf,df->rd', grad_pre, weight_in, preferred_e...  59.5 us
    reduce_scatter x1, waiting for transfers between devices, on_device(): lax.psum_scatter(jnp.dot(context, weight_out, preferred_element_type=f32)...  57.3 us
    psum x1, waiting for transfers between devices, on_device(): lax.psum(grad_weight_qkv.astype(jnp.bfloat16), 'dp').astype(jnp.float32)  52.3 us
    reduce_scatter x1, waiting for transfers between devices, on_device(): lax.psum_scatter(jnp.dot(lax.slice_in_dim(hidden_act, 0, tok_rows * lax.a...  46.3 us
    psum x1, blocking collectives, on_device(): lax.psum((count_local, grad_gain_one, grad_shift_one, grad_bias_out, grad...  41.3 us
    all_to_all x1, blocking collectives, _wait_limits(): lax.all_to_all(jnp.stack(tray), mesh_dim, 0, 0)  40.6 us
    all_gather x1, waiting for transfers between devices, on_device(): lax.all_gather(grad_h1.astype(bf16), 'mp', axis=0, tiled=True)  36.6 us
    all_gather x1, waiting for transfers between devices, on_device(): lax.all_gather(first_out.astype(bf16), 'mp', axis=0, tiled=True)  35.5 us
  transfers between devices with their start and end apart: 10, of which 8 were waited for; matrix products, arithmetic and copies ran while one was open for 7% of the time, Pallas kernels for 0%

profile of v1, /device:TPU:0, one launch (start us, length us, event | category | flops | bytes accessed | tf_op | source)
XLA Modules:
  0.0 691.3 jit_solution(10659765033091142563)
XLA Ops:
  11.9 14.3 %all_to_all.24 = s32[32,1,16]{2,1,0:T(1,128)S(1)} all-to-all(s32[32,1,16]{2,1,0:T(1,128)S(1)} %bitcast.201), channel_id=1, replica_groups=mesh['dp'=8,'mp'=4] {'dp','mp'}, dimensions={0} | all-to-all | bytes 4096 | tf_op jit(solution)/shard_map/all_to_all | solution.py:74
  26.5 14.0 %gather_fusion = bf16[512,768]{1,0:T(8,128)(2,1)} fusion(bf16[15664,768]{1,0:T(8,128)(2,1)} %param.27, s32[1024]{0:T(1024)S(1)} %pad_clamp_fusion.1), kind=kCustom, calls=%fused_computation | custom fusion | bytes 1574912 | tf_op jit(solution)/shard_map/gather | solution.py:80
  43.4 19.4 %all-to-all-done.1 = bf16[32,16,768]{2,1,0:T(8,128)(2,1)S(1)} async-done(((bf16[32,16,768]{2,1,0:T(8,128)(2,1)}), bf16[32,16,768]{2,1,0:T(8,128)(2,1)S(1)}, u32[]{:S(2)}, u32[]{:S(2)}) %all-to-all-start.1) | async-done | bytes 786464 | tf_op jit(solution)/shard_map/all_to_all | solution.py:79
  67.4 12.0 %all-reduce = bf16[16]{0:T(256)(128)(2,1)S(1)} all-reduce(bf16[16]{0:T(256)(128)(2,1)S(1)} %dynamic-update-slice), channel_id=1, replica_groups=mesh['dp'=8,'mp'=4] {'mp'}, use_global_device_ids=true, to_apply=%add | all-reduce | flops 16 | bytes 64
  80.2 21.7 %all-gather.9.cloned.1.call-done = bf16[1024,768]{1,0:T(8,128)(2,1)} async-done(((bf16[256,768]{1,0:T(8,128)(2,1)}), bf16[1024,768]{1,0:T(8,128)(2,1)}) %all-gather.9.cloned.1.call-update) | async-done | bytes 1572880 | tf_op jit(solution)/shard_map/all_gather | solution.py:98
  114.7 4.8 while.24
  127.6 57.3 %reduce-scatter.5.cloned.1.call-done = f32[256,768]{1,0:T(8,128)} async-done(((f32[1024,768]{1,0:T(8,128)}), f32[256,768]{1,0:T(8,128)}) %reduce-scatter.5.cloned.1.call-update) | async-done | bytes 786448 | tf_op jit(solution)/shard_map/reduce_scatter | solution.py:142
  190.3 35.5 %all-gather.5.cloned.1.call-done = bf16[1024,768]{1,0:T(8,128)(2,1)} async-done(((bf16[256,768]{1,0:T(8,128)(2,1)}), bf16[1024,768]{1,0:T(8,128)(2,1)}) %all-gather.5.cloned.1.call-update) | async-done | bytes 1572880 | tf_op jit(solution)/shard_map/all_gather | solution.py:153
  225.9 10.6 %multiply_convert_fusion.1 = (bf16[1024,768]{1,0:T(8,128)(2,1)S(1)}, f32[1024,768]{1,0:T(8,128)}, f32[1024,768]{1,0:T(8,128)}) fusion(f32[768]{0:T(1024)} %convert_element_type.189, bf16[1024,768]{1,0:T(8,128)(2,1)} %all-gather.5.cloned.1.call-done, bf16[768,768]{1,0:T(8,128)(2,1)S(1)} %copy-done), kind=kOutput, calls=%fused_computation.71 | convolution fusion | flops 1259864064 | bytes 10619904 | tf_op jit(solution)/shard_map/dot_general | solution.py:154
  253.9 46.3 %reduce-scatter.7.cloned.1.call-done = f32[256,768]{1,0:T(8,128)} async-done(((f32[1024,768]{1,0:T(8,128)}), f32[256,768]{1,0:T(8,128)}) %reduce-scatter.7.cloned.1.call-update) | async-done | bytes 786448 | tf_op jit(solution)/shard_map/reduce_scatter | solution.py:157
  305.8 40.6 %all_to_all.25 = bf16[4,256,768]{2,1,0:T(8,128)(2,1)S(1)} all-to-all(bf16[4,256,768]{2,1,0:T(8,128)(2,1)S(1)} %stack.19), channel_id=1, replica_groups=mesh['dp'=8,'mp'=4] {'mp'}, dimensions={0} | all-to-all | bytes 3145728 | tf_op jit(solution)/shard_map/all_to_all | solution.py:17
  353.6 59.5 %reduce-scatter.9.cloned.1.call-done = f32[256,768]{1,0:T(8,128)} async-done(((f32[1024,768]{1,0:T(8,128)}), f32[256,768]{1,0:T(8,128)}) %reduce-scatter.9.cloned.1.call-update) | async-done | bytes 786448 | tf_op jit(solution)/shard_map/reduce_scatter | solution.py:184
  417.5 36.6 %all-gather.7.cloned.1.call-done = bf16[1024,768]{1,0:T(8,128)(2,1)} async-done(((bf16[256,768]{1,0:T(8,128)(2,1)}), bf16[1024,768]{1,0:T(8,128)(2,1)}) %all-gather.7.cloned.1.call-update) | async-done | bytes 1572880 | tf_op jit(solution)/shard_map/all_gather | solution.py:194
  456.8 16.8 %while.25 = (s32[]{:T(128)}, bf16[2,8,64,3,3,64]{5,2,3,1,4,0:T(8,128)(2,1)}, bf16[2,8,64,3,64]{4,2,3,1,0:T(8,128)(2,1)S(1)}, f32[2,8]{1,0:T(2,128)S(1)}, bf16[2,...) while((s32[]{:T(128)}, ...), condition=%wide.region_23.24_spmd.clone, body=%wide.region_21.23_spmd.clone.sunk | while | flops 66059264 | bytes 22653772 | solution.py:221
  473.6 4.6 copy.153
  478.1 3.5 reshape.325
  481.6 3.9 convolution_convert_fusion.2
  486.3 4.0 convolution_convert_fusion.3
  492.9 41.3 %all-reduce.1 = (f32[]{:T(128)}, f32[768]{0:T(1024)S(1)}, f32[768]{0:T(1024)S(1)}, f32[768]{0:T(1024)S(1)}, f32[768]{0:T(1024)S(1)}, /*index=5*/f32[768]{0:T(1024)S(1)}, f32[768]{0:T(1024)S(1)}) all-reduce(f32[]{:T(128)S(6)} %convert_element_type.207, f32[768]{0:T(1024)S(1)} %copy-done.30, ...), channel_id=1, replica_groups=mesh['dp'=8,'mp'=4] {'dp','mp'}, use_global_device_ids=true, to_apply=%region_28.29 | all-reduce | flops 4609 | bytes 36872 | tf_op jit(solution)/shard_map/psum | solution.py:245
  537.3 3.4 convolution_convert_fusion.5
  545.5 13.9 %all-reduce.2 = (bf16[192]{0:T(256)(128)(2,1)S(1)}, bf16[192]{0:T(256)(128)(2,1)S(1)}, bf16[768]{0:T(1024)(128)(2,1)S(1)}) all-reduce(bf16[192]{0:T(256)(128)(2,1)S(1)} %convert_element_type.211, bf16[192]{0:T(256)(128)(2,1)S(1)} %convert_element_type.213, bf16[768]{0:T(1024)(128)(2,1)S(1)} %copy-done.37), channel_id=1, replica_groups=mesh['dp'=8,'mp'=4] {'dp'}, use_global_device_ids=true, to_apply=%region_31.32 | all-reduce | flops 1152 | bytes 4608 | tf_op jit(solution)/shard_map/psum | solution.py:260
  567.3 52.3 %all-reduce.6.cloned.1.call-done = (bf16[768,576]{0,1:T(8,128)(2,1)}, bf16[192,768]{1,0:T(8,128)(2,1)}, bf16[768,768]{1,0:T(8,128)(2,1)}, bf16[768,768]{1,0:T(8,128)(2,1)}) async-done(((bf16[768,576]{0,1:T(8,128)(2,1)}, bf16[192,768]{1,0:T(8,128)(2,1)}, bf16[768,768]{1,0:T(8,128)(2,1)}, bf16[768,768]{1,0:T(8,128)(2,1)}), (bf16[768,576]{0,1:T(8,128)(2,1)}, bf16[192,768]{1,0:T(8,128)(2,1)}, ...) | async-done | bytes 3538960 | tf_op jit(solution)/shard_map/psum | solution.py:259
  627.5 23.7 %scatter_custom_fusion.2 = f32[15664,768]{1,0:T(8,128)} fusion(s32[512]{0:T(512)} %copy-done.33, f32[512,768]{1,0:T(8,128)S(1)} %bitcast.200, f32[]{:T(128)} %constant.48.clone.1), kind=kCustom, calls=%fused_computation.66 | custom fusion | flops 393216 | bytes 48120320 | tf_op jit(solution)/shard_map/scatter-add | solution.py:279
  651.2 33.1 %broadcast_multiply_fusion = f32[15664,768]{1,0:T(8,128)} fusion(f32[15664,768]{1,0:T(8,128)} %scatter_custom_fusion.2, f32[]{:T(128)S(6)} %rsqrt.21), kind=kLoop, calls=%fused_computation.65 | loop fusion | flops 12029952 | bytes 96239616 | tf_op jit(solution)/shard_map/mul | solution.py:279
  (287 shorter events, 122.6 us)
Async XLA Ops:
  7.2 218.7 %copy-start = (bf16[768,768]{1,0:T(8,128)(2,1)S(1)}, bf16[768,768]{1,0:T(8,128)(2,1)}, u32[]{:S(2)}) copy-start(bf16[768,768]{1,0:T(8,128)(2,1)} %param.35) | copy-start | bytes 3538948
  40.5 39.5 %copy-start.38 = (bf16[192]{0:T(256)(128)(2,1)S(1)}, bf16[192]{0:T(256)(128)(2,1)}, u32[]{:S(2)}) copy-start(bf16[192]{0:T(256)(128)(2,1)} %param.29) | copy-start | bytes 1156
  40.5 39.6 %copy-start.39 = (bf16[192]{0:T(256)(128)(2,1)S(1)}, bf16[192]{0:T(256)(128)(2,1)}, u32[]{:S(2)}) copy-start(bf16[192]{0:T(256)(128)(2,1)} %param.30) | copy-start | bytes 1156
  40.5 61.3 %copy-start.44 = (bf16[768,576]{0,1:T(8,128)(2,1)S(1)}, bf16[768,576]{0,1:T(8,128)(2,1)}, u32[]{:S(2)}) copy-start(bf16[768,576]{0,1:T(8,128)(2,1)} %param.28) | copy-start | bytes 2654212
  40.5 22.3 %all-to-all-start.1 = ((bf16[32,16,768]{2,1,0:T(8,128)(2,1)}), bf16[32,16,768]{2,1,0:T(8,128)(2,1)S(1)}, u32[]{:S(2)}, u32[]{:S(2)}) async-start(bf16[32,16,768]{2,1,0:T(8,128)(2,1)} %bitcast.6), calls=%async_computation.1 | async-start | bytes 1572864 | tf_op jit(solution)/shard_map/all_to_all | solution.py:79
  43.3 58.5 %all-gather.9.cloned.1.call-start = ((), (), s32[]{:S(2)}) async-start(), calls=%async_computation.14 | async-start | bytes 1966080 | tf_op jit(solution)/shard_map/all_gather | solution.py:98
  64.7 120.2 %reduce-scatter.5.cloned.1.call-start = ((), (), s32[]{:S(2)}) async-start(), calls=%async_computation.8 | async-start | bytes 3932160 | tf_op jit(solution)/shard_map/reduce_scatter | solution.py:142
  125.6 100.3 %all-gather.5.cloned.1.call-start = ((), (), s32[]{:S(2)}) async-start(), calls=%async_computation.9 | async-start | bytes 1966080 | tf_op jit(solution)/shard_map/all_gather | solution.py:153
  188.8 111.4 %reduce-scatter.7.cloned.1.call-start = ((), (), s32[]{:S(2)}) async-start(), calls=%async_computation.10 | async-start | bytes 3932160 | tf_op jit(solution)/shard_map/reduce_scatter | solution.py:157
  240.8 172.3 %reduce-scatter.9.cloned.1.call-start = ((), (), s32[]{:S(2)}) async-start(), calls=%async_computation.11 | async-start | bytes 3932160 | tf_op jit(solution)/shard_map/reduce_scatter | solution.py:184
  303.0 43.4 %copy-start.52 = (f32[1024,768]{1,0:T(8,128)S(1)}, f32[1024,768]{1,0:T(8,128)}, u32[]{:S(2)}) copy-start(f32[1024,768]{1,0:T(8,128)} %get-tuple-element.298) | copy-start | bytes 9437188
  305.6 40.7 %copy-start.35 = (f32[768]{0:T(1024)S(1)}, f32[768]{0:T(1024)}, u32[]{:S(2)}) copy-start(f32[768]{0:T(1024)} %convert_element_type.189) | copy-start | bytes 9220
  305.6 40.7 %copy-start.43 = (bf16[768,768]{1,0:T(8,128)(2,1)S(1)}, bf16[768,768]{1,0:T(8,128)(2,1)}, u32[]{:S(2)}) copy-start(bf16[768,768]{1,0:T(8,128)(2,1)} %param.37) | copy-start | bytes 3538948
  305.6 40.7 %copy-start.51 = (f32[1024,768]{1,0:T(8,128)S(1)}, f32[1024,768]{1,0:T(8,128)}, u32[]{:S(2)}) copy-start(f32[1024,768]{1,0:T(8,128)} %get-tuple-element.281) | copy-start | bytes 9437188
  353.5 59.6 %copy-start.10 = (f32[256,768]{1,0:T(8,128)S(1)}, f32[256,768]{1,0:T(8,128)}, u32[]{:S(2)}) copy-start(f32[256,768]{1,0:T(8,128)} %copy-done.9) | copy-start | bytes 2359300
  353.5 59.6 %copy-start.24 = (f32[256]{0:T(256)S(1)}, f32[256]{0:T(256)}, u32[]{:S(2)}) copy-start(f32[256]{0:T(256)} %copy-done.23) | copy-start | bytes 3076
  353.5 100.6 %all-gather.7.cloned.1.call-start = ((), (), s32[]{:S(2)}) async-start(), calls=%async_computation.12 | async-start | bytes 1966080 | tf_op jit(solution)/shard_map/all_gather | solution.py:194
  416.2 38.0 %copy-start.7 = (f32[256,768]{1,0:T(8,128)}, f32[256,768]{1,0:T(8,128)S(1)}, u32[]{:S(2)}) copy-start(f32[256,768]{1,0:T(8,128)S(1)} %get-tuple-element.276) | copy-start | bytes 2359300
  416.2 40.6 %copy-start.46 = (f32[2,8]{1,0:T(2,128)S(1)}, f32[2,8]{1,0:T(2,128)}, u32[]{:S(2)}) copy-start(f32[2,8]{1,0:T(2,128)} %reshape.329) | copy-start | bytes 196
  417.1 142.9 %reduce-scatter.11.cloned.1.call-start = ((), (), s32[]{:S(2)}) async-start(), calls=%async_computation.13 | async-start | bytes 1966080 | tf_op jit(solution)/shard_map/reduce_scatter | solution.py:229
  485.5 134.1 %all-reduce.6.cloned.1.call-start = ((), (), s32[]{:S(2)}) async-start(), calls=%async_computation.15 | async-start | bytes 7077888 | tf_op jit(solution)/shard_map/psum | solution.py:259
  490.4 45.7 %copy-start.11 = (bf16[1024,192]{0,1:T(8,128)(2,1)S(1)}, bf16[1024,192]{0,1:T(8,128)(2,1)}, u32[]{:S(2)}) copy-start(bf16[1024,192]{0,1:T(8,128)(2,1)} %reshape.320) | copy-start | bytes 1179652
  490.4 45.7 %copy-start.14 = (bf16[1024,768]{1,0:T(8,128)(2,1)S(1)}, bf16[1024,768]{1,0:T(8,128)(2,1)}, u32[]{:S(2)}) copy-start(bf16[1024,768]{1,0:T(8,128)(2,1)} %all-gather.7.cloned.1.call-done) | copy-start | bytes 4718596
  563.3 63.9 %all-to-all-start.3 = ((bf16[32,16,768]{2,1,0:T(8,128)(2,1)}), bf16[32,16,768]{2,1,0:T(8,128)(2,1)S(1)}, u32[]{:S(2)}, u32[]{:S(2)}) async-start(bf16[32,16,768]{2,1,0:T(8,128)(2,1)} %bitcast.13), calls=%async_computation.7 | async-start | bytes 1572864 | tf_op jit(solution)/shard_map/all_to_all | solution.py:273
  (47 other events, 255.9 us)
Sparse Core Ops, SparseCore 0:
  64.9 36.9 all-gather.8
  125.7 59.2 reduce-scatter.4
  188.9 36.9 all-gather.4
  240.9 59.2 reduce-scatter.6
  353.6 59.4 reduce-scatter.8
  417.2 36.9 all-gather.6
  485.6 35.0 reduce-scatter.10
  540.9 78.6 all-reduce.5
